TPU v7x, 256 devices: a whole 4x4x8 slice. The times are simulated.
256 devices in a mesh: wide: 16 (over z_hi, x), narrow: 16 (over z_lo, y, core).
Axes of the slice: x: 4, y: 4, z: 8 (z_hi: 4, z_lo: 2; z = z_hi * 2 + z_lo), core: 2. Of those that a mesh axis runs over, the one named last changes fastest.
Arguments:
- node: bfloat16 [256, 256, 256], P('narrow'), may hold values from -6 to 6
- right_side: bfloat16 [256, 256, 256], P('narrow'), may hold values from -16 to 16
- leg_ops: bfloat16 [3, 12, 256, 256], replicated, may hold values from -0.375 to 0.375
- op_index: int32 [64, 3], P('wide'), may hold values from 0 to 11, as said below
- offsets: int32 [64], P('wide'), may hold values from 0 to 7
Outputs:
- new_node: float32 [256, 256, 256], P('narrow')
Inputs may be any that keep to these rules, and one draw needn't show every extreme that they name: `op_index`: no two triples name the same pair of leg b and leg c operators; every operator of each leg is named by some triple.
All inputs are finite; a program needn't handle non-finite values.
Results may differ from a plain program's by a relative error of at most 0.0019.
Values may be sent and summed in bfloat16 or wider, within the bound.
No kernel may reach another device: no remote copies, remote signals or barrier semaphores. Data moves between devices by JAX's collectives and lax.ppermute only.
A program may use at most 64 MiB of HBM per device.

v0:
```python
import math
import jax
import jax.numpy as jnp
from jax import lax
from jax.sharding import PartitionSpec as P

SECTORS = 8


def two_legs(rounded, leg_ops, op_index, triple):
    op_b = leg_ops[1, op_index[triple, 1]]
    op_c = leg_ops[2, op_index[triple, 2]]
    first = jnp.einsum("abc,qc->abq", rounded, op_c, preferred_element_type=jnp.float32).astype(
        jnp.bfloat16
    )
    return jnp.einsum("pb,abq->paq", op_b, first, preferred_element_type=jnp.float32).astype(
        jnp.bfloat16
    )


def third_leg(regrouped, leg_ops, op_index, offsets, triple, sector):
    op_a = jnp.roll(leg_ops[0, op_index[triple, 0]], offsets[triple] * sector, axis=0)
    return jnp.einsum("ra,paq->rpq", op_a, regrouped, preferred_element_type=jnp.float32)


def per_device(node, right_side, leg_ops, op_index, offsets):
    bond = node.shape[1]
    sector = bond // SECTORS
    trip_local = op_index.shape[0]
    tau = 0.5 / math.sqrt(trip_local * lax.axis_size("wide"))
    partial_value = None
    for triple in range(trip_local):
        second = two_legs(node, leg_ops, op_index, triple)
        regrouped = lax.all_to_all(second, "narrow", split_axis=0, concat_axis=1, tiled=True)
        term = third_leg(regrouped, leg_ops, op_index, offsets, triple, sector)
        partial_value = term if partial_value is None else partial_value + term
    back = lax.all_to_all(partial_value, "narrow", split_axis=0, concat_axis=1, tiled=True)
    sigma = lax.psum(back, "wide")
    return node.astype(jnp.float32) + tau * (right_side.astype(jnp.float32) - sigma)


def solution(mesh):
    in_specs = (P("narrow", None, None), P("narrow", None, None), P(), P("wide", None), P("wide"))
    out_specs = P("narrow", None, None)
    return jax.shard_map(
        per_device, mesh=mesh, in_specs=in_specs, out_specs=out_specs, check_vma=False
    )
```

profile of v0, /device:TPU:8, one launch (start us, length us, event | category | flops | bytes accessed | tf_op | source)
XLA Modules:
  0.0 456.6 jit_solution(17279808986567162240)
XLA Ops:
  6.5 1.8 fusion.99
  12.3 3.2 fusion.26
  15.5 2.5 copy.15
  18.0 0.0 copy-start
  18.0 6.5 %all-to-all-start.2 = ((bf16[256,16,256]{2,1,0:T(8,128)(2,1)}), bf16[256,16,256]{2,1,0:T(8,128)(2,1)}, u32[]{:S(2)}, u32[]{:S(2)}) async-start(bf16[256,16,256]{2,1,0:T(8,128)(2,1)} %copy.15), calls=%async_computation.2 | async-start | bytes 4194304 | tf_op jit(solution)/shard_map/all_to_all | solution.py:34
  28.1 0.0 copy-done
  28.1 3.8 fusion.23
  31.8 4.1 copy.13
  36.0 15.6 %all-to-all-done.2 = bf16[256,16,256]{2,1,0:T(8,128)(2,1)} async-done(((bf16[256,16,256]{2,1,0:T(8,128)(2,1)}), bf16[256,16,256]{2,1,0:T(8,128)(2,1)}, u32[]{:S(2)}, u32[]{:S(2)}) %all-to-all-start.2) | async-done | bytes 2097184 | tf_op jit(solution)/shard_map/all_to_all | solution.py:34
  51.6 6.8 %all-to-all-start.1 = ((bf16[256,16,256]{2,1,0:T(8,128)(2,1)}), bf16[256,16,256]{2,1,0:T(8,128)(2,1)}, u32[]{:S(2)}, u32[]{:S(2)}) async-start(bf16[256,16,256]{2,1,0:T(8,128)(2,1)} %copy.13), calls=%async_computation.1 | async-start | bytes 4194304 | tf_op jit(solution)/shard_map/all_to_all | solution.py:34
  62.1 3.8 fusion.20
  65.9 4.1 copy.11
  70.0 15.5 %all-to-all-done.1 = bf16[256,16,256]{2,1,0:T(8,128)(2,1)} async-done(((bf16[256,16,256]{2,1,0:T(8,128)(2,1)}), bf16[256,16,256]{2,1,0:T(8,128)(2,1)}, u32[]{:S(2)}, u32[]{:S(2)}) %all-to-all-start.1) | async-done | bytes 2097184 | tf_op jit(solution)/shard_map/all_to_all | solution.py:34
  85.5 6.8 %all-to-all-start = ((bf16[256,16,256]{2,1,0:T(8,128)(2,1)}), bf16[256,16,256]{2,1,0:T(8,128)(2,1)}, u32[]{:S(2)}, u32[]{:S(2)}) async-start(bf16[256,16,256]{2,1,0:T(8,128)(2,1)} %copy.11), calls=%async_computation | async-start | bytes 4194304 | tf_op jit(solution)/shard_map/all_to_all | solution.py:34
  95.9 3.8 fusion.29
  99.6 4.1 copy.17
  103.8 0.0 copy-start.4
  103.8 15.7 %all-to-all-done = bf16[256,16,256]{2,1,0:T(8,128)(2,1)} async-done(((bf16[256,16,256]{2,1,0:T(8,128)(2,1)}), bf16[256,16,256]{2,1,0:T(8,128)(2,1)}, u32[]{:S(2)}, u32[]{:S(2)}) %all-to-all-start) | async-done | bytes 2097184 | tf_op jit(solution)/shard_map/all_to_all | solution.py:34
  119.5 6.8 %all-to-all-start.3 = ((bf16[256,16,256]{2,1,0:T(8,128)(2,1)}), bf16[256,16,256]{2,1,0:T(8,128)(2,1)}, u32[]{:S(2)}, u32[]{:S(2)}) async-start(bf16[256,16,256]{2,1,0:T(8,128)(2,1)} %copy.17), calls=%async_computation.3 | async-start | bytes 4194304 | tf_op jit(solution)/shard_map/all_to_all | solution.py:34
  126.3 0.2 all-reduce.2.cloned.1.call-start
  126.5 0.0 copy-done.4
  126.5 0.7 fusion.100
  137.3 1.1 dynamic-slice_bitcast_fusion
  138.4 3.1 copy.16
  141.6 3.1 copy.14
  144.7 3.1 copy.12
  147.9 5.6 %all-to-all-done.3 = bf16[256,16,256]{2,1,0:T(8,128)(2,1)} async-done(((bf16[256,16,256]{2,1,0:T(8,128)(2,1)}), bf16[256,16,256]{2,1,0:T(8,128)(2,1)}, u32[]{:S(2)}, u32[]{:S(2)}) %all-to-all-start.3) | async-done | bytes 2097184 | tf_op jit(solution)/shard_map/all_to_all | solution.py:34
  153.4 0.0 copy-start.3
  153.5 1.9 copy.18
  155.4 0.3 copy-done.3
  155.7 0.0 copy-start.2
  155.7 0.9 fusion.37
  156.6 0.7 copy-done.2
  157.3 0.0 copy-start.1
  157.3 0.9 fusion.41
  158.1 0.7 copy-done.1
  158.9 0.9 fusion.45
  159.7 1.1 add_add_fusion
  160.9 2.4 copy.19
  163.3 53.1 %all_to_all.90 = f32[256,16,256]{2,1,0:T(8,128)S(1)} all-to-all(f32[256,16,256]{2,1,0:T(8,128)S(1)} %copy.19), channel_id=1, replica_groups=mesh['wide'=16,'narrow'=16] {'narrow'}, dimensions={0} | all-to-all | bytes 8388608 | tf_op jit(solution)/shard_map/all_to_all | solution.py:37
  216.4 2.6 copy.20
  219.0 0.0 all-reduce.2.cloned.1.call-update
  219.1 225.0 %all-reduce.2.cloned.1.call-done = f32[16,256,256]{2,1,0:T(8,128)} async-done(((f32[16,256,256]{2,1,0:T(8,128)}), f32[16,256,256]{2,1,0:T(8,128)}) %all-reduce.2.cloned.1.call-update) | async-done | bytes 4194320 | tf_op jit(solution)/shard_map/psum | solution.py:38
  444.1 5.7 %multiply_add_fusion = f32[16,256,256]{2,1,0:T(8,128)} fusion(f32[16,256,256]{2,1,0:T(8,128)} %all-reduce.2.cloned.1.call-done, bf16[16,256,256]{2,1,0:T(8,128)(2,1)} %param.8, bf16[16,256,256]{2,1,0:T(8,128)(2,1)S(1)} %copy-done), kind=kLoop, calls=%fused_computation | loop fusion | flops 5242880 | bytes 12582912 | tf_op jit(solution)/shard_map/add | solution.py:39
Async XLA Ops:
  18.0 10.1 %copy-start = (bf16[16,256,256]{2,1,0:T(8,128)(2,1)S(1)}, bf16[16,256,256]{2,1,0:T(8,128)(2,1)}, u32[]{:S(2)}) copy-start(bf16[16,256,256]{2,1,0:T(8,128)(2,1)} %param.7) | copy-start | bytes 6291460
  18.0 33.5 %all-to-all-start.2 = ((bf16[256,16,256]{2,1,0:T(8,128)(2,1)}), bf16[256,16,256]{2,1,0:T(8,128)(2,1)}, u32[]{:S(2)}, u32[]{:S(2)}) async-start(bf16[256,16,256]{2,1,0:T(8,128)(2,1)} %copy.15), calls=%async_computation.2 | async-start | bytes 4194304 | tf_op jit(solution)/shard_map/all_to_all | solution.py:34
  51.6 34.0 %all-to-all-start.1 = ((bf16[256,16,256]{2,1,0:T(8,128)(2,1)}), bf16[256,16,256]{2,1,0:T(8,128)(2,1)}, u32[]{:S(2)}, u32[]{:S(2)}) async-start(bf16[256,16,256]{2,1,0:T(8,128)(2,1)} %copy.13), calls=%async_computation.1 | async-start | bytes 4194304 | tf_op jit(solution)/shard_map/all_to_all | solution.py:34
  85.5 34.0 %all-to-all-start = ((bf16[256,16,256]{2,1,0:T(8,128)(2,1)}), bf16[256,16,256]{2,1,0:T(8,128)(2,1)}, u32[]{:S(2)}, u32[]{:S(2)}) async-start(bf16[256,16,256]{2,1,0:T(8,128)(2,1)} %copy.11), calls=%async_computation | async-start | bytes 4194304 | tf_op jit(solution)/shard_map/all_to_all | solution.py:34
  103.8 22.7 %copy-start.4 = (s32[4]{0:T(128)S(1)}, s32[4]{0:T(128)}, u32[]{:S(2)}) copy-start(s32[4]{0:T(128)} %param.11) | copy-start | bytes 52
  119.5 34.0 %all-to-all-start.3 = ((bf16[256,16,256]{2,1,0:T(8,128)(2,1)}), bf16[256,16,256]{2,1,0:T(8,128)(2,1)}, u32[]{:S(2)}, u32[]{:S(2)}) async-start(bf16[256,16,256]{2,1,0:T(8,128)(2,1)} %copy.17), calls=%async_computation.3 | async-start | bytes 4194304 | tf_op jit(solution)/shard_map/all_to_all | solution.py:34
  126.3 317.8 %all-reduce.2.cloned.1.call-start = ((), (), s32[]{:S(2)}) async-start(), calls=%async_computation.5 | async-start | bytes 8388608 | tf_op jit(solution)/shard_map/psum | solution.py:38
  153.4 2.2 copy-start.3
  155.7 1.6 copy-start.2
  157.3 1.6 copy-start.1
Sparse Core Ops, SparseCore 0:
  219.2 224.8 all-reduce.1
where the time goes:
time: 458 us; the launch traced here: 457 us
  waiting for transfers between devices  277 us (60%)
  blocking collectives  53.1 us (12%)
  between operations  38.6 us (8%)
  local copies, waits for them, and re-layouts  36.6 us (8%)
  starting transfers between devices  27 us (6%)
  matrix products  18.2 us (4%)
  other arithmetic  5.71 us (1%)
    psum x1, waiting for transfers between devices, per_device(): sigma = lax.psum(back, 'wide')  225 us
    all_to_all x1, blocking collectives, per_device(): lax.all_to_all(partial_value, 'narrow', split_axis=0, concat_axis=1, tile...  53.1 us
    all_to_all x4, waiting for transfers between devices, per_device(): lax.all_to_all(second, 'narrow', split_axis=0, concat_axis=1, tiled=True)  52.4 us
    all_to_all x4, starting transfers between devices, per_device(): lax.all_to_all(second, 'narrow', split_axis=0, concat_axis=1, tiled=True)  26.8 us
    convert_element_type x4, local copies, waits for them, and re-layouts, two_legs(): jnp.einsum('pb,abq->paq', op_b, first, preferred_element_type=jnp.float32)  14.9 us
    dot_general x4, matrix products, two_legs(): jnp.einsum('pb,abq->paq', op_b, first, preferred_element_type=jnp.float32)  14.5 us
    all_to_all x4, local copies, waits for them, and re-layouts, per_device(): lax.all_to_all(second, 'narrow', split_axis=0, concat_axis=1, tiled=True)  11.4 us
  transfers between devices with their start and end apart: 5, of which 5 were waited for; matrix products, arithmetic and copies ran while one was open for 8% of the time, Pallas kernels for 0%

commit v1 on v0

--- a/solution.py
+++ b/solution.py
@@ -34,7 +34,12 @@
         regrouped = lax.all_to_all(second, "narrow", split_axis=0, concat_axis=1, tiled=True)
         term = third_leg(regrouped, leg_ops, op_index, offsets, triple, sector)
         partial_value = term if partial_value is None else partial_value + term
-    back = lax.all_to_all(partial_value, "narrow", split_axis=0, concat_axis=1, tiled=True)
+    back = jnp.concatenate(
+        lax.all_to_all(
+            jnp.stack(jnp.split(partial_value, lax.axis_size("narrow"), axis=0)), "narrow", 0, 0
+        ),
+        axis=1,
+    )
     sigma = lax.psum(back, "wide")
     return node.astype(jnp.float32) + tau * (right_side.astype(jnp.float32) - sigma)
 

time: 458 us -> 460 us (level)
  no operation moved by 1% of the time
where the time goes in v1:
time: 460 us; the launch traced here: 459 us
  waiting for transfers between devices  277 us (60%)
  blocking collectives  53.1 us (12%)
  between operations  38.9 us (8%)
  local copies, waits for them, and re-layouts  37.5 us (8%)
  starting transfers between devices  26.9 us (6%)
  matrix products  19.5 us (4%)
  other arithmetic  5.71 us (1%)
    psum x1, waiting for transfers between devices, per_device(): sigma = lax.psum(back, 'wide')  225 us
    all_to_all x1, blocking collectives, per_device(): lax.all_to_all(jnp.stack(jnp.split(partial_value, lax.axis_size('narrow')...  53.1 us
    all_to_all x4, waiting for transfers between devices, per_device(): lax.all_to_all(second, 'narrow', split_axis=0, concat_axis=1, tiled=True)  52 us
    all_to_all x4, starting transfers between devices, per_device(): lax.all_to_all(second, 'narrow', split_axis=0, concat_axis=1, tiled=True)  26.6 us
    convert_element_type x4, local copies, waits for them, and re-layouts, two_legs(): jnp.einsum('pb,abq->paq', op_b, first, preferred_element_type=jnp.float32)  16.6 us
    dot_general x4, matrix products, two_legs(): jnp.einsum('pb,abq->paq', op_b, first, preferred_element_type=jnp.float32)  15.8 us
    all_to_all x4, local copies, waits for them, and re-layouts, per_device(): lax.all_to_all(second, 'narrow', split_axis=0, concat_axis=1, tiled=True)  11.4 us
  transfers between devices with their start and end apart: 5, of which 5 were waited for; matrix products, arithmetic and copies ran while one was open for 8% of the time, Pallas kernels for 0%

profile of v1, /device:TPU:8, one launch (start us, length us, event | category | flops | bytes accessed | tf_op | source)
XLA Modules:
  0.0 458.7 jit_solution(5560028829223326391)
XLA Ops:
  6.5 1.8 fusion.115
  12.2 4.5 fusion.26
  16.7 0.0 copy-start
  16.7 4.2 copy.15
  20.9 6.3 %all-to-all-start.2 = ((bf16[256,16,256]{2,1,0:T(8,128)(2,1)}), bf16[256,16,256]{2,1,0:T(8,128)(2,1)}, u32[]{:S(2)}, u32[]{:S(2)}) async-start(bf16[256,16,256]{2,1,0:T(8,128)(2,1)} %copy.15), calls=%async_computation.2 | async-start | bytes 4194304 | tf_op jit(solution)/shard_map/all_to_all | solution.py:34
  31.2 0.0 copy-done
  31.3 3.8 fusion.23
  35.0 4.1 copy.13
  39.1 15.2 %all-to-all-done.2 = bf16[256,16,256]{2,1,0:T(8,128)(2,1)} async-done(((bf16[256,16,256]{2,1,0:T(8,128)(2,1)}), bf16[256,16,256]{2,1,0:T(8,128)(2,1)}, u32[]{:S(2)}, u32[]{:S(2)}) %all-to-all-start.2) | async-done | bytes 2097184 | tf_op jit(solution)/shard_map/all_to_all | solution.py:34
  54.4 6.8 %all-to-all-start.1 = ((bf16[256,16,256]{2,1,0:T(8,128)(2,1)}), bf16[256,16,256]{2,1,0:T(8,128)(2,1)}, u32[]{:S(2)}, u32[]{:S(2)}) async-start(bf16[256,16,256]{2,1,0:T(8,128)(2,1)} %copy.13), calls=%async_computation.1 | async-start | bytes 4194304 | tf_op jit(solution)/shard_map/all_to_all | solution.py:34
  64.9 3.8 fusion.20
  68.7 4.1 copy.11
  72.8 15.5 %all-to-all-done.1 = bf16[256,16,256]{2,1,0:T(8,128)(2,1)} async-done(((bf16[256,16,256]{2,1,0:T(8,128)(2,1)}), bf16[256,16,256]{2,1,0:T(8,128)(2,1)}, u32[]{:S(2)}, u32[]{:S(2)}) %all-to-all-start.1) | async-done | bytes 2097184 | tf_op jit(solution)/shard_map/all_to_all | solution.py:34
  88.3 6.8 %all-to-all-start = ((bf16[256,16,256]{2,1,0:T(8,128)(2,1)}), bf16[256,16,256]{2,1,0:T(8,128)(2,1)}, u32[]{:S(2)}, u32[]{:S(2)}) async-start(bf16[256,16,256]{2,1,0:T(8,128)(2,1)} %copy.11), calls=%async_computation | async-start | bytes 4194304 | tf_op jit(solution)/shard_map/all_to_all | solution.py:34
  98.7 3.8 fusion.29
  102.4 0.0 copy-start.4
  102.4 4.1 copy.17
  106.6 15.7 %all-to-all-done = bf16[256,16,256]{2,1,0:T(8,128)(2,1)} async-done(((bf16[256,16,256]{2,1,0:T(8,128)(2,1)}), bf16[256,16,256]{2,1,0:T(8,128)(2,1)}, u32[]{:S(2)}, u32[]{:S(2)}) %all-to-all-start) | async-done | bytes 2097184 | tf_op jit(solution)/shard_map/all_to_all | solution.py:34
  122.3 6.8 %all-to-all-start.3 = ((bf16[256,16,256]{2,1,0:T(8,128)(2,1)}), bf16[256,16,256]{2,1,0:T(8,128)(2,1)}, u32[]{:S(2)}, u32[]{:S(2)}) async-start(bf16[256,16,256]{2,1,0:T(8,128)(2,1)} %copy.17), calls=%async_computation.3 | async-start | bytes 4194304 | tf_op jit(solution)/shard_map/all_to_all | solution.py:34
  129.1 0.2 all-reduce.2.cloned.1.call-start
  129.3 0.0 copy-done.4
  129.3 0.7 fusion.116
  140.1 1.1 dynamic-slice_bitcast_fusion
  141.2 3.1 copy.16
  144.4 3.1 copy.14
  147.5 3.1 copy.12
  150.7 5.6 %all-to-all-done.3 = bf16[256,16,256]{2,1,0:T(8,128)(2,1)} async-done(((bf16[256,16,256]{2,1,0:T(8,128)(2,1)}), bf16[256,16,256]{2,1,0:T(8,128)(2,1)}, u32[]{:S(2)}, u32[]{:S(2)}) %all-to-all-start.3) | async-done | bytes 2097184 | tf_op jit(solution)/shard_map/all_to_all | solution.py:34
  156.3 0.0 copy-start.3
  156.3 1.9 copy.18
  158.2 0.0 copy-start.2
  158.2 0.3 copy-done.3
  158.5 0.9 fusion.53
  159.4 0.0 copy-start.1
  159.4 0.5 copy-done.2
  159.9 0.9 fusion.57
  160.7 0.3 copy-done.1
  161.1 0.9 fusion.61
  162.0 1.1 add_add_fusion
  163.5 53.1 %all_to_all.77 = f32[16,16,16,256]{3,1,2,0:T(8,128)S(1)} all-to-all(f32[16,16,16,256]{3,1,2,0:T(8,128)S(1)} %fusion.32), channel_id=1, replica_groups=mesh['wide'=16,'narrow'=16] {'narrow'}, dimensions={0} | all-to-all | bytes 8388608 | tf_op jit(solution)/shard_map/all_to_all | solution.py:38
  216.6 4.4 copy.19
  221.1 0.0 all-reduce.2.cloned.1.call-update
  221.1 225.0 %all-reduce.2.cloned.1.call-done = f32[16,256,256]{2,1,0:T(8,128)} async-done(((f32[16,256,256]{2,1,0:T(8,128)}), f32[16,256,256]{2,1,0:T(8,128)}) %all-reduce.2.cloned.1.call-update) | async-done | bytes 4194320 | tf_op jit(solution)/shard_map/psum | solution.py:43
  446.1 5.7 %multiply_add_fusion = f32[16,256,256]{2,1,0:T(8,128)} fusion(f32[16,256,256]{2,1,0:T(8,128)} %all-reduce.2.cloned.1.call-done, bf16[16,256,256]{2,1,0:T(8,128)(2,1)} %param.8, bf16[16,256,256]{2,1,0:T(8,128)(2,1)S(1)} %copy-done), kind=kLoop, calls=%fused_computation | loop fusion | flops 5242880 | bytes 12582912 | tf_op jit(solution)/shard_map/add | solution.py:44
  (16 shorter events, 0.3 us)
Async XLA Ops:
  16.7 14.5 %copy-start = (bf16[16,256,256]{2,1,0:T(8,128)(2,1)S(1)}, bf16[16,256,256]{2,1,0:T(8,128)(2,1)}, u32[]{:S(2)}) copy-start(bf16[16,256,256]{2,1,0:T(8,128)(2,1)} %param.7) | copy-start | bytes 6291460
  20.9 33.4 %all-to-all-start.2 = ((bf16[256,16,256]{2,1,0:T(8,128)(2,1)}), bf16[256,16,256]{2,1,0:T(8,128)(2,1)}, u32[]{:S(2)}, u32[]{:S(2)}) async-start(bf16[256,16,256]{2,1,0:T(8,128)(2,1)} %copy.15), calls=%async_computation.2 | async-start | bytes 4194304 | tf_op jit(solution)/shard_map/all_to_all | solution.py:34
  54.4 34.0 %all-to-all-start.1 = ((bf16[256,16,256]{2,1,0:T(8,128)(2,1)}), bf16[256,16,256]{2,1,0:T(8,128)(2,1)}, u32[]{:S(2)}, u32[]{:S(2)}) async-start(bf16[256,16,256]{2,1,0:T(8,128)(2,1)} %copy.13), calls=%async_computation.1 | async-start | bytes 4194304 | tf_op jit(solution)/shard_map/all_to_all | solution.py:34
  88.3 34.0 %all-to-all-start = ((bf16[256,16,256]{2,1,0:T(8,128)(2,1)}), bf16[256,16,256]{2,1,0:T(8,128)(2,1)}, u32[]{:S(2)}, u32[]{:S(2)}) async-start(bf16[256,16,256]{2,1,0:T(8,128)(2,1)} %copy.11), calls=%async_computation | async-start | bytes 4194304 | tf_op jit(solution)/shard_map/all_to_all | solution.py:34
  102.4 26.8 %copy-start.4 = (s32[4]{0:T(128)S(1)}, s32[4]{0:T(128)}, u32[]{:S(2)}) copy-start(s32[4]{0:T(128)} %param.11) | copy-start | bytes 52
  122.3 34.0 %all-to-all-start.3 = ((bf16[256,16,256]{2,1,0:T(8,128)(2,1)}), bf16[256,16,256]{2,1,0:T(8,128)(2,1)}, u32[]{:S(2)}, u32[]{:S(2)}) async-start(bf16[256,16,256]{2,1,0:T(8,128)(2,1)} %copy.17), calls=%async_computation.3 | async-start | bytes 4194304 | tf_op jit(solution)/shard_map/all_to_all | solution.py:34
  129.1 317.0 %all-reduce.2.cloned.1.call-start = ((), (), s32[]{:S(2)}) async-start(), calls=%async_computation.5 | async-start | bytes 8388608 | tf_op jit(solution)/shard_map/psum | solution.py:43
  156.3 2.2 copy-start.3
  158.2 1.7 copy-start.2
  159.4 1.7 copy-start.1
Sparse Core Ops, SparseCore 0:
  221.2 224.8 all-reduce.1
